TPU v7x, 32 devices: a whole 2x2x4 slice. The times are simulated.
32 devices in a mesh: cp: 4 (over y, x), grp: 8 (over z, core).
Axes of the slice: x: 2, y: 2, z: 4, core: 2. Of those that a mesh axis runs over, the one named last changes fastest.
Arguments:
- queries: bfloat16 [16, 512, 2048], P('grp', 'cp'), may hold values from -108 to 108
- keys: bfloat16 [16, 512, 2048], P('grp', 'cp'), may hold values from -4 to 4
- values: bfloat16 [16, 512, 2048], P('grp', 'cp'), may hold values from -6 to 6
- lengths: int32 [16], P('grp'), may hold values from 128 to 512
- frame_map: bfloat16 [2048, 2176], replicated, may hold values from -0.125 to 0.125
- proj_weight: bfloat16 [2176, 4096], P('grp', 'cp'), may hold values from -0.125 to 0.125
- head_weight: bfloat16 [4096, 256], P('cp'), may hold values from -0.375 to 0.375
- act_embed: float32 [7, 4096], P(None, 'cp'), may hold values from -0.5 to 0.5
- actions: int32 [16, 7], P('grp'), may hold values from 0 to 255
- action_mask: int32 [16, 7], P('grp'), may hold values 0 or 1
- group_ids: int32 [16], P('grp'), may hold values from 0 to 1
- rewards: float32 [16], P('grp'), may hold values from -6 to 6
Outputs:
- logprobs: float32 [16, 7], P('grp')
- grad_proj: bfloat16 [2176, 4096], P('grp', 'cp')
- grad_head: bfloat16 [4096, 256], P('cp')
All inputs are finite; a program needn't handle non-finite values. No bound on the sum of `action_mask` on one device may be relied on, other than what follows from the above.
Results may differ from a plain program's by a relative error of at most 0.018.
Values may be sent and summed in bfloat16 or wider, within the bound.
A program may use at most 128 MiB of HBM per device.

v0:
```python
import math
import jax
import jax.numpy as jnp
from jax import lax
from jax.sharding import PartitionSpec as P

HD = 128
SQRT_HALF = 0.7071067811865476
INV_ROOT_TAU = 0.3989422804014327
NEG_LARGE = -1e30


def gelu_exact(values_in):
    return 0.5 * values_in * (1.0 + lax.erf(values_in * SQRT_HALF))


def gelu_slope(values_in):
    return (
        0.5 * (1.0 + lax.erf(values_in * SQRT_HALF))
        + values_in * jnp.exp(-0.5 * values_in * values_in) * INV_ROOT_TAU
    )


def fetch_columns(proj_weight):
    return lax.all_gather(proj_weight, "grp", axis=0, tiled=True)


def attention(queries, keys, values, lengths):
    episodes_here, tokens_here, att_width = queries.shape
    head_count = att_width // HD
    query_heads = queries.reshape(episodes_here, tokens_here, head_count, HD)
    key_heads = keys.reshape(episodes_here, tokens_here, head_count, HD)
    value_heads = values.reshape(episodes_here, tokens_here, head_count, HD)
    query_all, key_all, value_all = (
        lax.all_to_all(query_heads, "cp", split_axis=2, concat_axis=1, tiled=True),
        lax.all_to_all(key_heads, "cp", split_axis=2, concat_axis=1, tiled=True),
        lax.all_to_all(value_heads, "cp", split_axis=2, concat_axis=1, tiled=True),
    )
    seq_span = query_all.shape[1]
    scores = jnp.einsum(
        "eihd,ejhd->ehij", query_all, key_all, preferred_element_type=jnp.float32
    ) / math.sqrt(HD)
    live_keys = (jnp.arange(seq_span, dtype=jnp.int32)[None, :] < lengths[:, None])[
        :, None, None, :
    ]
    scores = jnp.where(live_keys, scores, NEG_LARGE)
    row_max = jnp.max(scores, axis=-1, keepdims=True)
    probs = jnp.where(live_keys, jnp.exp(scores - row_max), 0.0)
    row_total = jnp.sum(probs, axis=-1)
    weighted = jnp.einsum(
        "ehij,ejhd->eihd", probs.astype(jnp.bfloat16), value_all, preferred_element_type=jnp.float32
    )
    output = (weighted / jnp.transpose(row_total, (0, 2, 1))[..., None]).astype(jnp.bfloat16)
    returned = lax.all_to_all(output, "cp", split_axis=1, concat_axis=2, tiled=True)
    return returned.reshape(episodes_here, tokens_here, att_width)


def per_device(
    queries,
    keys,
    values,
    lengths,
    frame_map,
    proj_weight,
    head_weight,
    act_embed,
    actions,
    action_mask,
    group_ids,
    rewards,
):
    episodes_here, tokens_here, att_width = queries.shape
    action_count = act_embed.shape[0]
    lengths_real = lengths.astype(jnp.float32)
    attended = attention(queries, keys, values, lengths)
    proj_cols = fetch_columns(proj_weight)
    frames = jnp.dot(
        attended.reshape(episodes_here * tokens_here, att_width),
        frame_map,
        preferred_element_type=jnp.float32,
    )
    frames = frames.astype(jnp.bfloat16).reshape(episodes_here, tokens_here, frame_map.shape[1])
    all_frames = lax.all_gather(frames, "cp", axis=1, tiled=True)
    seq_span = all_frames.shape[1]
    flat_frames = all_frames.reshape(episodes_here * seq_span, all_frames.shape[2])
    col_count = proj_cols.shape[1]
    pre_act = jnp.dot(flat_frames, proj_cols, preferred_element_type=jnp.float32).reshape(
        episodes_here, seq_span, col_count
    )
    hidden = gelu_exact(pre_act)
    token_mask = (jnp.arange(seq_span, dtype=jnp.int32)[None, :] < lengths[:, None]).astype(
        jnp.float32
    )
    pooled = jnp.sum(token_mask[:, :, None] * hidden, axis=1) / lengths_real[:, None]
    sum_input = pooled[:, None, :] + act_embed[None, :, :]
    head_input = sum_input.astype(jnp.bfloat16).reshape(episodes_here * action_count, col_count)
    partial_logits = jnp.dot(head_input, head_weight, preferred_element_type=jnp.float32)
    episodes_total = episodes_here * lax.axis_size("grp")
    group_count = max(1, episodes_total // 8)
    membership = (group_ids[:, None] == jnp.arange(group_count, dtype=jnp.int32)[None, :]).astype(
        jnp.float32
    )
    masked = action_mask.astype(jnp.float32)
    logits = lax.psum(partial_logits, "cp")
    reward_sums, squares, group_sizes, mask_total = lax.psum(
        (
            jnp.sum(membership * rewards[:, None], axis=0),
            jnp.sum(membership * (rewards * rewards)[:, None], axis=0),
            jnp.sum(membership, axis=0),
            jnp.sum(masked),
        ),
        "grp",
    )
    log_all = jax.nn.log_softmax(logits, axis=-1)
    bin_ids = jnp.arange(head_weight.shape[1], dtype=jnp.int32)
    picked = (actions.reshape(-1)[:, None] == bin_ids[None, :]).astype(jnp.float32)
    logprobs = jnp.sum(picked * log_all, axis=-1).reshape(episodes_here, action_count)
    size_floor = jnp.maximum(group_sizes, 1.0)
    group_mean = reward_sums / size_floor
    variance = squares / size_floor - group_mean * group_mean
    group_scale = jnp.sqrt(jnp.maximum(variance, 1.0))
    advantage = (rewards - jnp.sum(membership * group_mean[None, :], axis=1)) / jnp.sum(
        membership * group_scale[None, :], axis=1
    )
    loss_weight = (-masked * advantage[:, None] / jnp.maximum(mask_total, 1.0)).reshape(-1)
    logit_grad = (loss_weight[:, None] * (picked - jnp.exp(log_all))).astype(jnp.bfloat16)
    head_term = lax.dot_general(
        head_input, logit_grad, (((0,), (0,)), ((), ())), preferred_element_type=jnp.float32
    )
    grad_head = lax.psum(head_term.astype(jnp.bfloat16), "grp")
    pull_back = lax.dot_general(
        logit_grad, head_weight, (((1,), (1,)), ((), ())), preferred_element_type=jnp.float32
    )
    pool_grad = jnp.sum(pull_back.reshape(episodes_here, action_count, col_count), axis=1)
    scaled_mask = token_mask / lengths_real[:, None]
    act_grad = (scaled_mask[:, :, None] * pool_grad[:, None, :] * gelu_slope(pre_act)).astype(
        jnp.bfloat16
    )
    act_flat = act_grad.reshape(episodes_here * seq_span, col_count)
    grad_proj = lax.psum_scatter(
        lax.dot_general(
            flat_frames, act_flat, (((0,), (0,)), ((), ())), preferred_element_type=jnp.float32
        ).astype(jnp.bfloat16),
        "grp",
        scatter_dimension=0,
        tiled=True,
    )
    return (logprobs, grad_proj, grad_head)


def solution(mesh):
    in_specs = (
        P("grp", "cp", None),
        P("grp", "cp", None),
        P("grp", "cp", None),
        P("grp"),
        P(),
        P("grp", "cp"),
        P("cp", None),
        P(None, "cp"),
        P("grp", None),
        P("grp", None),
        P("grp"),
        P("grp"),
    )
    out_specs = (P("grp", None), P("grp", "cp"), P("cp", None))
    return jax.shard_map(
        per_device, mesh=mesh, in_specs=in_specs, out_specs=out_specs, check_vma=False
    )
```

profile of v0, /device:TPU:0, one launch (start us, length us, event | category | flops | bytes accessed | tf_op | source)
XLA Modules:
  0.0 302.5 jit_solution(11430559681268954911)
XLA Ops:
  7.2 0.7 all-gather.5.cloned.1.call-update
  7.9 1.6 copy.51
  9.5 1.0 copy.52
  10.6 5.2 %all-to-all-start = ((bf16[2,128,16,128]{1,3,0,2:T(8,128)(2,1)}), bf16[2,128,16,128]{1,3,0,2:T(8,128)(2,1)S(1)}, u32[]{:S(2)}, u32[]{:S(2)}) async-start(bf16[2,128,16,128]{1,3,0,2:T(8,128)(2,1)} %copy.52), calls=%async_computation | async-start | bytes 2097152 | tf_op jit(solution)/shard_map/all_to_all | solution.py:35
  15.8 1.6 copy.55
  17.4 1.1 copy.56
  18.5 10.9 %all-to-all-done = bf16[2,128,16,128]{1,3,0,2:T(8,128)(2,1)S(1)} async-done(((bf16[2,128,16,128]{1,3,0,2:T(8,128)(2,1)}), bf16[2,128,16,128]{1,3,0,2:T(8,128)(2,1)S(1)}, u32[]{:S(2)}, u32[]{:S(2)}) %all-to-all-start) | async-done | bytes 1048608 | tf_op jit(solution)/shard_map/all_to_all | solution.py:35
  29.4 3.5 %all-to-all-start.1 = ((bf16[2,128,16,128]{1,3,0,2:T(8,128)(2,1)}), bf16[2,128,16,128]{1,3,0,2:T(8,128)(2,1)S(1)}, u32[]{:S(2)}, u32[]{:S(2)}) async-start(bf16[2,128,16,128]{1,3,0,2:T(8,128)(2,1)} %copy.56), calls=%async_computation.1 | async-start | bytes 2097152 | tf_op jit(solution)/shard_map/all_to_all | solution.py:36
  32.9 2.3 copy.59
  35.2 2.3 copy.60
  37.5 8.6 %all-to-all-done.1 = bf16[2,128,16,128]{1,3,0,2:T(8,128)(2,1)S(1)} async-done(((bf16[2,128,16,128]{1,3,0,2:T(8,128)(2,1)}), bf16[2,128,16,128]{1,3,0,2:T(8,128)(2,1)S(1)}, u32[]{:S(2)}, u32[]{:S(2)}) %all-to-all-start.1) | async-done | bytes 1048608 | tf_op jit(solution)/shard_map/all_to_all | solution.py:36
  46.2 4.3 %all-to-all-start.2 = ((bf16[2,128,16,128]{1,3,0,2:T(8,128)(2,1)}), bf16[2,128,16,128]{1,3,0,2:T(8,128)(2,1)}, u32[]{:S(2)}, u32[]{:S(2)}) async-start(bf16[2,128,16,128]{1,3,0,2:T(8,128)(2,1)} %copy.60), calls=%async_computation.2 | async-start | bytes 2097152 | tf_op jit(solution)/shard_map/all_to_all | solution.py:37
  50.6 1.3 copy.54
  51.9 1.4 copy.58
  53.2 10.5 %all-to-all-done.2 = bf16[2,128,16,128]{1,3,0,2:T(8,128)(2,1)} async-done(((bf16[2,128,16,128]{1,3,0,2:T(8,128)(2,1)}), bf16[2,128,16,128]{1,3,0,2:T(8,128)(2,1)}, u32[]{:S(2)}, u32[]{:S(2)}) %all-to-all-start.2) | async-done | bytes 1048608 | tf_op jit(solution)/shard_map/all_to_all | solution.py:37
  63.7 1.6 copy.62
  65.4 6.8 %fusion.33 = (f32[2,4,512]{2,1,0:T(4,128)S(1)}, bf16[2,4,512,512]{2,3,1,0:T(8,128)(2,1)}) fusion(pred[2,512]{1,0:T(4,128)(4,1)S(1)} %get-tuple-element.15, bf16[2,512,4,128]{3,1,2,0:T(8,128)(2,1)S(1)} %bitcast.54, bf16[2,512,4,128]{3,1,2,0:T(8,128)(2,1)} %bitcast.55), kind=kOutput, calls=%fused_computation.58 | convolution fusion | flops 549454336 | bytes 6308864 | tf_op jit(solution)/shard_map/sub | solution.py:48
  72.2 3.9 %fusion.16 = bf16[2,512,4,128]{3,1,2,0:T(8,128)(2,1)S(1)} fusion(bf16[2,512,4,128]{3,1,2,0:T(8,128)(2,1)S(1)} %bitcast.56, bf16[2,4,512,512]{2,3,1,0:T(8,128)(2,1)} %get-tuple-element.17, f32[2,512,4]{1,2,0:T(4,128)S(1)} %bitcast.57), kind=kOutput, calls=%fused_computation.23 | convolution fusion | flops 537919488 | bytes 6307840 | tf_op jit(solution)/shard_map/ehij,ejhd->eihd/dot_general | solution.py:50
  76.1 0.8 copy.64
  76.9 16.1 %all_to_all.69 = bf16[2,512,4,128]{3,2,0,1:T(4,128)(2,1)S(1)} all-to-all(bf16[2,512,4,128]{3,2,0,1:T(4,128)(2,1)S(1)} %copy.64), channel_id=1, replica_groups=mesh['cp'=4,'grp'=8] {'cp'}, dimensions={1} | all-to-all | bytes 2097152 | tf_op jit(solution)/shard_map/all_to_all | solution.py:54
  93.4 0.8 reshape_reshape.3
  94.3 7.2 %convolution_convert_fusion = bf16[256,2176]{1,0:T(8,128)(2,1)} fusion(bf16[256,2048]{1,0:T(8,128)(2,1)S(1)} %reshape_reshape.3, bf16[2048,2176]{1,0:T(8,128)(2,1)} %param.16), kind=kOutput, calls=%fused_computation.21 | convolution fusion | flops 2282258432 | bytes 11075584 | tf_op jit(solution)/shard_map/dot_general | solution.py:77
  102.3 15.2 %all-reduce = (f32[]{:T(128)}, f32[2]{0:T(128)S(1)}, f32[2]{0:T(128)S(1)}, f32[2]{0:T(128)S(1)}) all-reduce(f32[]{:T(128)} %convert_reduce_fusion.1, f32[2]{0:T(128)S(1)} %get-tuple-element.7, f32[2]{0:T(128)S(1)} %get-tuple-element.6, f32[2]{0:T(128)S(1)} %get-tuple-element.5), channel_id=1, replica_groups=mesh['cp'=4,'grp'=8] {'grp'}, use_global_device_ids=true, to_apply=%region_16.17 | all-reduce | flops 7 | bytes 56 | tf_op jit(solution)/shard_map/psum | solution.py:105
  118.7 37.5 %all-gather.3.cloned.1.call-done = bf16[2,512,2176]{2,1,0:T(8,128)(2,1)} async-done(((bf16[2,128,2176]{2,1,0:T(8,128)(2,1)}), bf16[2,512,2176]{2,1,0:T(8,128)(2,1)}) %all-gather.3.cloned.1.call-update) | async-done | bytes 4456464 | tf_op jit(solution)/shard_map/all_gather | solution.py:83
  156.2 9.9 %multiply_reduce_fusion = (f32[2,1024]{1,0:T(2,128)S(1)}, f32[2,512,1024]{2,1,0:T(8,128)}) fusion(f32[2,512]{1,0:T(2,128)S(1)} %get-tuple-element.14, bf16[2,512,2176]{2,1,0:T(8,128)(2,1)} %all-gather.3.cloned.1.call-done, bf16[2176,1024]{1,0:T(8,128)(2,1)} %all-gather.5.cloned.1.call-done), kind=kOutput, calls=%fused_computation.14 | convolution fusion | flops 4569692160 | bytes 13119488 | tf_op jit(solution)/shard_map/dot_general | solution.py:87
  166.4 15.1 %psum.42 = f32[14,256]{1,0:T(8,128)S(1)} all-reduce(f32[14,256]{1,0:T(8,128)S(1)} %fusion.34), channel_id=1, replica_groups=mesh['cp'=4,'grp'=8] {'cp'}, use_global_device_ids=true, to_apply=%region_3.4 | all-reduce | flops 3584 | bytes 28672 | tf_op jit(solution)/shard_map/psum | solution.py:104
  182.1 1.2 convolution_convert_fusion.1
  183.4 10.3 %bitcast_convert_fusion = bf16[2176,1024]{1,0:T(8,128)(2,1)} fusion(bf16[2,512,2176]{2,1,0:T(8,128)(2,1)} %all-gather.3.cloned.1.call-done, f32[2,512,1024]{2,1,0:T(8,128)} %get-tuple-element.19, f32[2,1024]{1,0:T(2,128)S(1)} %reduce_sum.110, f32[2,512]{1,0:T(2,128)S(1)} %broadcast_divide_fusion.1), kind=kOutput, calls=%fused_computation.1 | convolution fusion | flops 4577165312 | bytes 13119488 | tf_op jit(solution)/shard_map/dot_general | solution.py:141
  193.9 0.6 reshape.138
  194.5 45.4 %all-reduce.3.cloned.1.call-done = bf16[1024,256]{1,0:T(8,128)(2,1)} async-done(((bf16[1024,256]{1,0:T(8,128)(2,1)}), bf16[1024,256]{1,0:T(8,128)(2,1)}) %all-reduce.3.cloned.1.call-update) | async-done | bytes 524304 | tf_op jit(solution)/shard_map/psum | solution.py:130
  239.9 54.2 %reduce-scatter.2.cloned.1.call-done = bf16[272,1024]{1,0:T(8,128)(2,1)} async-done(((bf16[2176,1024]{1,0:T(8,128)(2,1)}), bf16[272,1024]{1,0:T(8,128)(2,1)}) %reduce-scatter.2.cloned.1.call-update) | async-done | bytes 557072 | tf_op jit(solution)/shard_map/reduce_scatter | solution.py:140
  294.1 1.9 copy.75
  (48 shorter events, 3.0 us)
Async XLA Ops:
  7.2 159.1 %copy-start = (bf16[1024,256]{1,0:T(8,128)(2,1)S(1)}, bf16[1024,256]{1,0:T(8,128)(2,1)}, u32[]{:S(2)}) copy-start(bf16[1024,256]{1,0:T(8,128)(2,1)} %param.18) | copy-start | bytes 1572868
  7.2 111.5 %all-gather.5.cloned.1.call-start = ((), (), s32[]{:S(2)}) async-start(), calls=%async_computation.6 | async-start | bytes 5013504 | tf_op jit(solution)/shard_map/all_gather | solution.py:25
  10.6 18.8 %all-to-all-start = ((bf16[2,128,16,128]{1,3,0,2:T(8,128)(2,1)}), bf16[2,128,16,128]{1,3,0,2:T(8,128)(2,1)S(1)}, u32[]{:S(2)}, u32[]{:S(2)}) async-start(bf16[2,128,16,128]{1,3,0,2:T(8,128)(2,1)} %copy.52), calls=%async_computation | async-start | bytes 2097152 | tf_op jit(solution)/shard_map/all_to_all | solution.py:35
  18.5 32.0 %copy-start.5 = (s32[2]{0:T(128)S(1)}, s32[2]{0:T(128)}, u32[]{:S(2)}) copy-start(s32[2]{0:T(128)} %param.15) | copy-start | bytes 28
  29.4 16.8 %all-to-all-start.1 = ((bf16[2,128,16,128]{1,3,0,2:T(8,128)(2,1)}), bf16[2,128,16,128]{1,3,0,2:T(8,128)(2,1)S(1)}, u32[]{:S(2)}, u32[]{:S(2)}) async-start(bf16[2,128,16,128]{1,3,0,2:T(8,128)(2,1)} %copy.56), calls=%async_computation.1 | async-start | bytes 2097152 | tf_op jit(solution)/shard_map/all_to_all | solution.py:36
  46.2 17.6 %all-to-all-start.2 = ((bf16[2,128,16,128]{1,3,0,2:T(8,128)(2,1)}), bf16[2,128,16,128]{1,3,0,2:T(8,128)(2,1)}, u32[]{:S(2)}, u32[]{:S(2)}) async-start(bf16[2,128,16,128]{1,3,0,2:T(8,128)(2,1)} %copy.60), calls=%async_computation.2 | async-start | bytes 2097152 | tf_op jit(solution)/shard_map/all_to_all | solution.py:37
  50.4 105.8 %all-gather.3.cloned.1.call-start = ((), (), s32[]{:S(2)}) async-start(), calls=%async_computation.5 | async-start | bytes 5570560 | tf_op jit(solution)/shard_map/all_gather | solution.py:83
  51.9 13.5 %copy-start.1 = (bf16[2,4,128,4,128]{4,2,1,3,0:T(8,128)(2,1)S(1)}, bf16[2,4,128,4,128]{4,2,1,3,0:T(8,128)(2,1)}, u32[]{:S(2)}) copy-start(bf16[2,4,128,4,128]{4,2,1,3,0:T(8,128)(2,1)} %copy.54) | copy-start | bytes 3145732
  94.2 7.3 %copy-start.4 = (f32[2]{0:T(128)S(1)}, f32[2]{0:T(128)}, u32[]{:S(2)}) copy-start(f32[2]{0:T(128)} %param.23) | copy-start | bytes 28
  94.2 7.4 %copy-start.6 = (s32[2,7]{1,0:T(2,128)S(1)}, s32[2,7]{1,0:T(2,128)}, u32[]{:S(2)}) copy-start(s32[2,7]{1,0:T(2,128)} %param.21) | copy-start | bytes 172
  94.2 8.0 %copy-start.3 = (s32[2]{0:T(128)S(1)}, s32[2]{0:T(128)}, u32[]{:S(2)}) copy-start(s32[2]{0:T(128)} %param.22) | copy-start | bytes 28
  94.3 23.3 %copy-start.7 = (s32[2,7]{1,0:T(2,128)S(1)}, s32[2,7]{1,0:T(2,128)}, u32[]{:S(2)}) copy-start(s32[2,7]{1,0:T(2,128)} %param.20) | copy-start | bytes 172
  101.5 138.4 %all-reduce.3.cloned.1.call-start = ((), (), s32[]{:S(2)}) async-start(), calls=%async_computation.8 | async-start | bytes 1048576 | tf_op jit(solution)/shard_map/psum | solution.py:130
  156.2 10.0 %copy-start.2 = (f32[7,1024]{1,0:T(8,128)S(1)}, f32[7,1024]{1,0:T(8,128)}, u32[]{:S(2)}) copy-start(f32[7,1024]{1,0:T(8,128)} %param.19) | copy-start | bytes 86020
  183.3 110.8 %reduce-scatter.2.cloned.1.call-start = ((), (), s32[]{:S(2)}) async-start(), calls=%async_computation.7 | async-start | bytes 5013504 | tf_op jit(solution)/shard_map/reduce_scatter | solution.py:140
Sparse Core Ops, SparseCore 0:
  9.6 51.7 all-gather.4
  101.6 54.4 all-gather.2
  183.4 56.4 all-reduce.2
  242.7 51.4 reduce-scatter.1
where the time goes:
time: 303 us
  waiting for transfers between devices  168 us (55%)
  blocking collectives  46.4 us (15%)
  matrix products  39.8 us (13%)
  local copies, waits for them, and re-layouts  19 us (6%)
  between operations  14.6 us (5%)
  starting transfers between devices  13.1 us (4%)
    reduce_scatter x1, waiting for transfers between devices, per_device(): lax.psum_scatter(lax.dot_general(flat_frames, act_flat, (((0,), (0,)), ((...  54.2 us
    psum x1, waiting for transfers between devices, per_device(): grad_head = lax.psum(head_term.astype(jnp.bfloat16), 'grp')  45.4 us
    all_gather x1, waiting for transfers between devices, per_device(): all_frames = lax.all_gather(frames, 'cp', axis=1, tiled=True)  37.5 us
    all_to_all x1, blocking collectives, attention(): lax.all_to_all(output, 'cp', split_axis=1, concat_axis=2, tiled=True)  16.1 us
    psum x1, blocking collectives, per_device(): lax.psum((jnp.sum(membership * rewards[:, None], axis=0), jnp.sum(members...  15.2 us
    psum x1, blocking collectives, per_device(): logits = lax.psum(partial_logits, 'cp')  15.1 us
    all_to_all x1, waiting for transfers between devices, attention(): lax.all_to_all(query_heads, 'cp', split_axis=2, concat_axis=1, tiled=True)  10.9 us
    all_to_all x1, waiting for transfers between devices, attention(): lax.all_to_all(value_heads, 'cp', split_axis=2, concat_axis=1, tiled=True)  10.5 us
  transfers between devices with their start and end apart: 7, of which 6 were waited for; matrix products, arithmetic and copies ran while one was open for 15% of the time, Pallas kernels for 0%

commit v1 on v0

--- a/solution.py
+++ b/solution.py
@@ -127,7 +127,7 @@
     head_term = lax.dot_general(
         head_input, logit_grad, (((0,), (0,)), ((), ())), preferred_element_type=jnp.float32
     )
-    grad_head = lax.psum(head_term.astype(jnp.bfloat16), "grp")
+    grad_head = jnp.sum(lax.all_gather(head_term.astype(jnp.bfloat16), "grp"), axis=0)
     pull_back = lax.dot_general(
         logit_grad, head_weight, (((1,), (1,)), ((), ())), preferred_element_type=jnp.float32
     )

time: 303 us -> 291 us (0.960)
  waiting for transfers between devices: 168 us -> 154 us
  other arithmetic: 1.73 us -> 5.43 us
    psum x1 -> x0, waiting for transfers between devices: 45.4 us -> none  [per_device(): grad_head = lax.psum(head_term.astype(jnp.bfloat16), 'grp')]
    all_gather x0 -> x1, waiting for transfers between devices: none -> 35.4 us  [per_device(): lax.all_gather(head_term.astype(jnp.bfloat16), 'grp')]
    reduce_scatter x1, waiting for transfers between devices: 54.2 us -> 50.3 us  [per_device(): lax.psum_scatter(lax.dot_general(flat_frames, act_flat, (((0,), (0,)), ((...]
    reduce_sum x0 -> x1, other arithmetic: none -> 3.7 us  [per_device(): jnp.sum(lax.all_gather(head_term.astype(jnp.bfloat16), 'grp'), axis=0)]
    unnamed x20 -> x19, local copies, waits for them, and re-layouts: 7.4 us -> 5.53 us
  transfers between devices with their start and end apart: 7 -> 7, of which waited for: 6 -> 6; matrix products, arithmetic and copies ran while one was open for 15% -> 17% of each run, Pallas kernels for 0% -> 0%
where the time goes in v1:
time: 291 us
  waiting for transfers between devices  154 us (53%)
  blocking collectives  46.4 us (16%)
  matrix products  39.7 us (14%)
  local copies, waits for them, and re-layouts  17.1 us (6%)
  between operations  14.6 us (5%)
  starting transfers between devices  13.1 us (5%)
  other arithmetic  5.43 us (2%)
    reduce_scatter x1, waiting for transfers between devices, per_device(): lax.psum_scatter(lax.dot_general(flat_frames, act_flat, (((0,), (0,)), ((...  50.3 us
    all_gather x1, waiting for transfers between devices, per_device(): all_frames = lax.all_gather(frames, 'cp', axis=1, tiled=True)  37.6 us
    all_gather x1, waiting for transfers between devices, per_device(): lax.all_gather(head_term.astype(jnp.bfloat16), 'grp')  35.4 us
    all_to_all x1, blocking collectives, attention(): lax.all_to_all(output, 'cp', split_axis=1, concat_axis=2, tiled=True)  16.1 us
    psum x1, blocking collectives, per_device(): lax.psum((jnp.sum(membership * rewards[:, None], axis=0), jnp.sum(members...  15.2 us
    psum x1, blocking collectives, per_device(): logits = lax.psum(partial_logits, 'cp')  15.1 us
    all_to_all x1, waiting for transfers between devices, attention(): lax.all_to_all(query_heads, 'cp', split_axis=2, concat_axis=1, tiled=True)  10.9 us
    all_to_all x1, waiting for transfers between devices, attention(): lax.all_to_all(value_heads, 'cp', split_axis=2, concat_axis=1, tiled=True)  10.5 us
  transfers between devices with their start and end apart: 7, of which 6 were waited for; matrix products, arithmetic and copies ran while one was open for 17% of the time, Pallas kernels for 0%

profile of v1, /device:TPU:0, one launch (start us, length us, event | category | flops | bytes accessed | tf_op | source)
XLA Modules:
  0.0 290.5 jit_solution(16228729840222325299)
XLA Ops:
  7.2 0.7 all-gather.7.cloned.1.call-update
  7.9 1.6 copy.51
  9.5 1.0 copy.52
  10.6 5.2 %all-to-all-start = ((bf16[2,128,16,128]{1,3,0,2:T(8,128)(2,1)}), bf16[2,128,16,128]{1,3,0,2:T(8,128)(2,1)S(1)}, u32[]{:S(2)}, u32[]{:S(2)}) async-start(bf16[2,128,16,128]{1,3,0,2:T(8,128)(2,1)} %copy.52), calls=%async_computation | async-start | bytes 2097152 | tf_op jit(solution)/shard_map/all_to_all | solution.py:35
  15.8 1.6 copy.55
  17.4 1.1 copy.56
  18.5 10.9 %all-to-all-done = bf16[2,128,16,128]{1,3,0,2:T(8,128)(2,1)S(1)} async-done(((bf16[2,128,16,128]{1,3,0,2:T(8,128)(2,1)}), bf16[2,128,16,128]{1,3,0,2:T(8,128)(2,1)S(1)}, u32[]{:S(2)}, u32[]{:S(2)}) %all-to-all-start) | async-done | bytes 1048608 | tf_op jit(solution)/shard_map/all_to_all | solution.py:35
  29.4 3.5 %all-to-all-start.1 = ((bf16[2,128,16,128]{1,3,0,2:T(8,128)(2,1)}), bf16[2,128,16,128]{1,3,0,2:T(8,128)(2,1)S(1)}, u32[]{:S(2)}, u32[]{:S(2)}) async-start(bf16[2,128,16,128]{1,3,0,2:T(8,128)(2,1)} %copy.56), calls=%async_computation.1 | async-start | bytes 2097152 | tf_op jit(solution)/shard_map/all_to_all | solution.py:36
  32.9 2.3 copy.59
  35.2 2.3 copy.60
  37.5 8.6 %all-to-all-done.1 = bf16[2,128,16,128]{1,3,0,2:T(8,128)(2,1)S(1)} async-done(((bf16[2,128,16,128]{1,3,0,2:T(8,128)(2,1)}), bf16[2,128,16,128]{1,3,0,2:T(8,128)(2,1)S(1)}, u32[]{:S(2)}, u32[]{:S(2)}) %all-to-all-start.1) | async-done | bytes 1048608 | tf_op jit(solution)/shard_map/all_to_all | solution.py:36
  46.2 4.3 %all-to-all-start.2 = ((bf16[2,128,16,128]{1,3,0,2:T(8,128)(2,1)}), bf16[2,128,16,128]{1,3,0,2:T(8,128)(2,1)}, u32[]{:S(2)}, u32[]{:S(2)}) async-start(bf16[2,128,16,128]{1,3,0,2:T(8,128)(2,1)} %copy.60), calls=%async_computation.2 | async-start | bytes 2097152 | tf_op jit(solution)/shard_map/all_to_all | solution.py:37
  50.6 1.3 copy.54
  51.9 1.4 copy.58
  53.2 10.5 %all-to-all-done.2 = bf16[2,128,16,128]{1,3,0,2:T(8,128)(2,1)} async-done(((bf16[2,128,16,128]{1,3,0,2:T(8,128)(2,1)}), bf16[2,128,16,128]{1,3,0,2:T(8,128)(2,1)}, u32[]{:S(2)}, u32[]{:S(2)}) %all-to-all-start.2) | async-done | bytes 1048608 | tf_op jit(solution)/shard_map/all_to_all | solution.py:37
  63.7 1.6 copy.62
  65.4 6.8 %fusion.33 = (f32[2,4,512]{2,1,0:T(4,128)S(1)}, bf16[2,4,512,512]{2,3,1,0:T(8,128)(2,1)}) fusion(pred[2,512]{1,0:T(4,128)(4,1)S(1)} %get-tuple-element.15, bf16[2,512,4,128]{3,1,2,0:T(8,128)(2,1)S(1)} %bitcast.56, bf16[2,512,4,128]{3,1,2,0:T(8,128)(2,1)} %bitcast.57), kind=kOutput, calls=%fused_computation.58 | convolution fusion | flops 549454336 | bytes 6308864 | tf_op jit(solution)/shard_map/sub | solution.py:48
  72.2 3.9 %fusion.16 = bf16[2,512,4,128]{3,1,2,0:T(8,128)(2,1)S(1)} fusion(bf16[2,512,4,128]{3,1,2,0:T(8,128)(2,1)S(1)} %bitcast.58, bf16[2,4,512,512]{2,3,1,0:T(8,128)(2,1)} %get-tuple-element.17, f32[2,512,4]{1,2,0:T(4,128)S(1)} %bitcast.59), kind=kOutput, calls=%fused_computation.23 | convolution fusion | flops 537919488 | bytes 6307840 | tf_op jit(solution)/shard_map/ehij,ejhd->eihd/dot_general | solution.py:50
  76.1 0.8 copy.64
  76.9 16.1 %all_to_all.69 = bf16[2,512,4,128]{3,2,0,1:T(4,128)(2,1)S(1)} all-to-all(bf16[2,512,4,128]{3,2,0,1:T(4,128)(2,1)S(1)} %copy.64), channel_id=1, replica_groups=mesh['cp'=4,'grp'=8] {'cp'}, dimensions={1} | all-to-all | bytes 2097152 | tf_op jit(solution)/shard_map/all_to_all | solution.py:54
  93.4 0.8 reshape_reshape.3
  94.3 7.2 %convolution_convert_fusion = bf16[256,2176]{1,0:T(8,128)(2,1)} fusion(bf16[256,2048]{1,0:T(8,128)(2,1)S(1)} %reshape_reshape.3, bf16[2048,2176]{1,0:T(8,128)(2,1)} %param.16), kind=kOutput, calls=%fused_computation.21 | convolution fusion | flops 2282258432 | bytes 11075584 | tf_op jit(solution)/shard_map/dot_general | solution.py:77
  102.3 15.2 %all-reduce = (f32[]{:T(128)}, f32[2]{0:T(128)S(1)}, f32[2]{0:T(128)S(1)}, f32[2]{0:T(128)S(1)}) all-reduce(f32[]{:T(128)} %convert_reduce_fusion.1, f32[2]{0:T(128)S(1)} %get-tuple-element.7, f32[2]{0:T(128)S(1)} %get-tuple-element.6, f32[2]{0:T(128)S(1)} %get-tuple-element.5), channel_id=1, replica_groups=mesh['cp'=4,'grp'=8] {'grp'}, use_global_device_ids=true, to_apply=%region_16.17 | all-reduce | flops 7 | bytes 56 | tf_op jit(solution)/shard_map/psum | solution.py:105
  118.6 37.6 %all-gather.5.cloned.1.call-done = bf16[2,512,2176]{2,1,0:T(8,128)(2,1)} async-done(((bf16[2,128,2176]{2,1,0:T(8,128)(2,1)}), bf16[2,512,2176]{2,1,0:T(8,128)(2,1)}) %all-gather.5.cloned.1.call-update) | async-done | bytes 4456464 | tf_op jit(solution)/shard_map/all_gather | solution.py:83
  156.2 9.9 %multiply_reduce_fusion = (f32[2,1024]{1,0:T(2,128)S(1)}, f32[2,512,1024]{2,1,0:T(8,128)}) fusion(f32[2,512]{1,0:T(2,128)S(1)} %get-tuple-element.14, bf16[2,512,2176]{2,1,0:T(8,128)(2,1)} %all-gather.5.cloned.1.call-done, bf16[2176,1024]{1,0:T(8,128)(2,1)} %all-gather.7.cloned.1.call-done), kind=kOutput, calls=%fused_computation.14 | convolution fusion | flops 4569692160 | bytes 13119488 | tf_op jit(solution)/shard_map/dot_general | solution.py:87
  166.4 15.1 %psum.35 = f32[14,256]{1,0:T(8,128)S(1)} all-reduce(f32[14,256]{1,0:T(8,128)S(1)} %fusion.34), channel_id=1, replica_groups=mesh['cp'=4,'grp'=8] {'cp'}, use_global_device_ids=true, to_apply=%region_3.4 | all-reduce | flops 3584 | bytes 28672 | tf_op jit(solution)/shard_map/psum | solution.py:104
  181.8 1.2 convolution_convert_fusion.1
  183.5 10.3 %bitcast_convert_fusion = bf16[2176,1024]{1,0:T(8,128)(2,1)} fusion(bf16[2,512,2176]{2,1,0:T(8,128)(2,1)} %all-gather.5.cloned.1.call-done, f32[2,512,1024]{2,1,0:T(8,128)} %get-tuple-element.19, f32[2,1024]{1,0:T(2,128)S(1)} %reduce_sum.122, f32[2,512]{1,0:T(2,128)S(1)} %broadcast_divide_fusion.1), kind=kOutput, calls=%fused_computation.1 | convolution fusion | flops 4577165312 | bytes 13119488 | tf_op jit(solution)/shard_map/dot_general | solution.py:141
  193.9 0.6 reshape.138
  194.6 35.4 %all-gather.9.cloned.1.call-done = bf16[8192,256]{1,0:T(8,128)(2,1)} async-done(((bf16[1024,256]{1,0:T(8,128)(2,1)}), bf16[8192,256]{1,0:T(8,128)(2,1)}) %all-gather.9.cloned.1.call-update) | async-done | bytes 4194320 | tf_op jit(solution)/shard_map/all_gather | solution.py:130
  230.0 3.7 %reduce_sum.123 = bf16[1024,256]{1,0:T(8,128)(2,1)} reduce(bf16[8,1024,256]{2,1,0:T(8,128)(2,1)} %bitcast.47, bf16[]{:T(256)} %constant.33.clone.1), dimensions={0}, to_apply=%region_19.20 | reduce | flops 1835008 | bytes 4718594 | tf_op jit(solution)/shard_map/reduce_sum | solution.py:130
  233.7 50.3 %reduce-scatter.2.cloned.1.call-done = bf16[272,1024]{1,0:T(8,128)(2,1)} async-done(((bf16[2176,1024]{1,0:T(8,128)(2,1)}), bf16[272,1024]{1,0:T(8,128)(2,1)}) %reduce-scatter.2.cloned.1.call-update) | async-done | bytes 557072 | tf_op jit(solution)/shard_map/reduce_scatter | solution.py:140
  (48 shorter events, 3.0 us)
Async XLA Ops:
  7.2 159.1 %copy-start = (bf16[1024,256]{1,0:T(8,128)(2,1)S(1)}, bf16[1024,256]{1,0:T(8,128)(2,1)}, u32[]{:S(2)}) copy-start(bf16[1024,256]{1,0:T(8,128)(2,1)} %param.18) | copy-start | bytes 1572868
  7.2 111.4 %all-gather.7.cloned.1.call-start = ((), (), s32[]{:S(2)}) async-start(), calls=%async_computation.6 | async-start | bytes 5013504 | tf_op jit(solution)/shard_map/all_gather | solution.py:25
  10.6 18.8 %all-to-all-start = ((bf16[2,128,16,128]{1,3,0,2:T(8,128)(2,1)}), bf16[2,128,16,128]{1,3,0,2:T(8,128)(2,1)S(1)}, u32[]{:S(2)}, u32[]{:S(2)}) async-start(bf16[2,128,16,128]{1,3,0,2:T(8,128)(2,1)} %copy.52), calls=%async_computation | async-start | bytes 2097152 | tf_op jit(solution)/shard_map/all_to_all | solution.py:35
  18.5 32.0 %copy-start.5 = (s32[2]{0:T(128)S(1)}, s32[2]{0:T(128)}, u32[]{:S(2)}) copy-start(s32[2]{0:T(128)} %param.15) | copy-start | bytes 28
  29.4 16.8 %all-to-all-start.1 = ((bf16[2,128,16,128]{1,3,0,2:T(8,128)(2,1)}), bf16[2,128,16,128]{1,3,0,2:T(8,128)(2,1)S(1)}, u32[]{:S(2)}, u32[]{:S(2)}) async-start(bf16[2,128,16,128]{1,3,0,2:T(8,128)(2,1)} %copy.56), calls=%async_computation.1 | async-start | bytes 2097152 | tf_op jit(solution)/shard_map/all_to_all | solution.py:36
  46.2 17.6 %all-to-all-start.2 = ((bf16[2,128,16,128]{1,3,0,2:T(8,128)(2,1)}), bf16[2,128,16,128]{1,3,0,2:T(8,128)(2,1)}, u32[]{:S(2)}, u32[]{:S(2)}) async-start(bf16[2,128,16,128]{1,3,0,2:T(8,128)(2,1)} %copy.60), calls=%async_computation.2 | async-start | bytes 2097152 | tf_op jit(solution)/shard_map/all_to_all | solution.py:37
  50.4 105.8 %all-gather.5.cloned.1.call-start = ((), (), s32[]{:S(2)}) async-start(), calls=%async_computation.5 | async-start | bytes 5570560 | tf_op jit(solution)/shard_map/all_gather | solution.py:83
  51.9 13.5 %copy-start.1 = (bf16[2,4,128,4,128]{4,2,1,3,0:T(8,128)(2,1)S(1)}, bf16[2,4,128,4,128]{4,2,1,3,0:T(8,128)(2,1)}, u32[]{:S(2)}) copy-start(bf16[2,4,128,4,128]{4,2,1,3,0:T(8,128)(2,1)} %copy.54) | copy-start | bytes 3145732
  94.2 7.3 %copy-start.4 = (f32[2]{0:T(128)S(1)}, f32[2]{0:T(128)}, u32[]{:S(2)}) copy-start(f32[2]{0:T(128)} %param.23) | copy-start | bytes 28
  94.2 7.4 %copy-start.6 = (s32[2,7]{1,0:T(2,128)S(1)}, s32[2,7]{1,0:T(2,128)}, u32[]{:S(2)}) copy-start(s32[2,7]{1,0:T(2,128)} %param.21) | copy-start | bytes 172
  94.2 8.0 %copy-start.3 = (s32[2]{0:T(128)S(1)}, s32[2]{0:T(128)}, u32[]{:S(2)}) copy-start(s32[2]{0:T(128)} %param.22) | copy-start | bytes 28
  94.3 23.3 %copy-start.7 = (s32[2,7]{1,0:T(2,128)S(1)}, s32[2,7]{1,0:T(2,128)}, u32[]{:S(2)}) copy-start(s32[2,7]{1,0:T(2,128)} %param.20) | copy-start | bytes 172
  101.5 128.5 %all-gather.9.cloned.1.call-start = ((), (), s32[]{:S(2)}) async-start(), calls=%async_computation.8 | async-start | bytes 4718592 | tf_op jit(solution)/shard_map/all_gather | solution.py:130
  156.2 10.0 %copy-start.2 = (f32[7,1024]{1,0:T(8,128)S(1)}, f32[7,1024]{1,0:T(8,128)}, u32[]{:S(2)}) copy-start(f32[7,1024]{1,0:T(8,128)} %param.19) | copy-start | bytes 86020
  183.0 101.0 %reduce-scatter.2.cloned.1.call-start = ((), (), s32[]{:S(2)}) async-start(), calls=%async_computation.7 | async-start | bytes 5013504 | tf_op jit(solution)/shard_map/reduce_scatter | solution.py:140
Sparse Core Ops, SparseCore 0:
  9.6 51.7 all-gather.6
  101.6 54.4 all-gather.4
  183.1 46.8 all-gather.8
  232.7 51.2 reduce-scatter.1
